TPU v7x, 256 devices: a whole 4x4x8 slice. The times are simulated.
256 devices in a mesh: own: 32 (over x_lo, z, core), blk: 8 (over x_hi, y).
Axes of the slice: x: 4 (x_hi: 2, x_lo: 2; x = x_hi * 2 + x_lo), y: 4, z: 8, core: 2. Of those that a mesh axis runs over, the one named last changes fastest.
Arguments:
- amplitudes: bfloat16 [32, 3072, 3072], P('own', 'blk'), may hold values from -6 to 6
- amp_mask: int32 [32, 24, 24], P('own', 'blk'), may hold values 0 or 1
- bare_ints: bfloat16 [32, 3072, 3072], P('own', 'blk'), may hold values from -6 to 6
- int_tiles: bfloat16 [8, 32, 10, 128, 128], P('blk', 'own'), may hold values from -0.125 to 0.125
- tile_ids: int32 [8, 32, 10], P('blk', 'own'), may hold values from -1 to 71, as said below
- eps_virt: float32 [3072], replicated, may hold values from 0.5 to 3
- eps_pair: float32 [32], P('own'), may hold values from -2 to -0.5
Outputs:
- new_amps: bfloat16 [32, 3072, 3072], P('own', 'blk')
Inputs may be any that keep to these rules, and one draw needn't show every extreme that they name: `tile_ids`: each entry is -1 or id = a * 24 + c for a live tile at row a of the block's 3 tile rows and column c; each position appears at most once in a block; each block of index g has exactly 64 live tiles, among them always the last position; no device holds more than 10, and in every block one device holds exactly 10.
All inputs are finite; a program needn't handle non-finite values. No bound on the sum of `amp_mask` on one device may be relied on, other than what follows from the above.
Results may differ from a plain program's by a relative error of at most 0.001.
Values may be sent and summed in bfloat16 or wider, within the bound.
A program may use at most 128 MiB of HBM per device.

v0:
```python
import jax
import jax.numpy as jnp
from jax import lax
from jax.sharding import PartitionSpec as P

TILE = 128
NT = 24


def passed_along(value, axis, steps):
    count = lax.axis_size(axis)
    pairs = [(source, (source + steps) % count) for source in range(count)]
    return lax.ppermute(value, axis, pairs)


def local(amplitudes, amp_mask, bare_ints, int_tiles, tile_ids, eps_virt, eps_pair):
    pairs, panel_rows, width = amplitudes.shape
    row_tiles = panel_rows // TILE
    slots = row_tiles * NT
    mask_cells = jnp.broadcast_to(
        amp_mask.astype(jnp.bfloat16)[:, :, None, :, None], (pairs, row_tiles, TILE, NT, TILE)
    ).reshape(pairs, panel_rows, width)
    screened = amplitudes * mask_cells
    tiles = lax.all_gather(int_tiles, "own", axis=1, tiled=True)
    labels = lax.all_gather(tile_ids, "own", axis=1, tiled=True)
    flat_labels = labels.reshape(-1)
    flat_tiles = tiles.reshape(-1, TILE, TILE)
    onehot = (flat_labels[:, None] == jnp.arange(slots, dtype=jnp.int32)[None, :]).astype(
        jnp.bfloat16
    )
    grid = jnp.einsum("sq,sij->qij", onehot, flat_tiles, preferred_element_type=jnp.float32)
    w_rows = (
        grid.astype(jnp.bfloat16)
        .reshape(row_tiles, NT, TILE, TILE)
        .transpose(0, 2, 1, 3)
        .reshape(panel_rows, width)
    )
    position = lax.axis_index("blk")
    stops = lax.axis_size("blk")
    panel = screened
    cycle_sum = jnp.zeros((pairs, panel_rows, width), jnp.float32)
    for stop in range(stops):
        columns = lax.dynamic_slice_in_dim(
            w_rows, (position - stop) % stops * panel_rows, panel_rows, 1
        )
        cycle_sum = cycle_sum + jnp.einsum(
            "ac,pcb->pab", columns, panel, preferred_element_type=jnp.float32
        )
        if stop + 1 < stops:
            panel = passed_along(panel, "blk", 1)
    rows_energy = lax.dynamic_slice_in_dim(eps_virt, position * panel_rows, panel_rows, 0)
    denom = rows_energy[None, :, None] + eps_virt[None, None, :] - eps_pair[:, None, None]
    updated = (bare_ints.astype(jnp.float32) + cycle_sum) / denom * mask_cells.astype(jnp.float32)
    return updated.astype(jnp.bfloat16)


def solution(mesh):
    in_specs = (
        P("own", "blk", None),
        P("own", "blk", None),
        P("own", "blk", None),
        P("blk", "own", None, None, None),
        P("blk", "own", None),
        P(),
        P("own"),
    )
    out_specs = P("own", "blk", None)
    return jax.shard_map(local, mesh=mesh, in_specs=in_specs, out_specs=out_specs, check_vma=False)
```

profile of v0, /device:TPU:2, one launch (start us, length us, event | category | flops | bytes accessed | tf_op | source)
XLA Modules:
  0.0 470.2 jit_solution(8401497030724276519)
XLA Ops:
  6.5 0.7 all-gather.2.cloned.1.call-update
  7.3 0.7 convert_element_type.25
  7.9 1.8 broadcast_in_dim.7
  9.7 3.6 broadcast_in_dim.16
  13.4 2.5 mul.33
  15.9 0.0 copy-start
  15.9 1.4 copy-done
  17.3 1.6 collective-permute-start
  18.9 101.4 %collective-permute-done = bf16[1,384,3072]{2,1,0:T(8,128)(2,1)S(1)} collective-permute-done((bf16[1,384,3072]{2,1,0:T(8,128)(2,1)S(1)}, bf16[1,384,3072]{2,1,0:T(8,128)(2,1)S(1)}, u32[]{:S(2)}, u32[]{:S(2)}) %collective-permute-start) | collective-permute-done | bytes 2359328 | tf_op jit(solution)/shard_map/ppermute | solution.py:13
  120.2 1.4 copy-done.3
  121.6 0.0 collective-permute-start.1
  121.6 55.5 %collective-permute-done.1 = bf16[1,384,3072]{2,1,0:T(8,128)(2,1)S(1)} collective-permute-done((bf16[1,384,3072]{2,1,0:T(8,128)(2,1)S(1)}, bf16[1,384,3072]{2,1,0:T(8,128)(2,1)S(1)}, u32[]{:S(2)}, u32[]{:S(2)}) %collective-permute-start.1) | collective-permute-done | bytes 2359328 | tf_op jit(solution)/shard_map/ppermute | solution.py:13
  177.1 1.4 copy-done.5
  178.6 0.0 collective-permute-start.2
  178.6 54.6 %collective-permute-done.2 = bf16[1,384,3072]{2,1,0:T(8,128)(2,1)S(1)} collective-permute-done((bf16[1,384,3072]{2,1,0:T(8,128)(2,1)S(1)}, bf16[1,384,3072]{2,1,0:T(8,128)(2,1)S(1)}, u32[]{:S(2)}, u32[]{:S(2)}) %collective-permute-start.2) | collective-permute-done | bytes 2359328 | tf_op jit(solution)/shard_map/ppermute | solution.py:13
  233.1 1.4 copy-done.7
  234.6 0.0 collective-permute-start.3
  234.6 53.6 %collective-permute-done.3 = bf16[1,384,3072]{2,1,0:T(8,128)(2,1)S(1)} collective-permute-done((bf16[1,384,3072]{2,1,0:T(8,128)(2,1)S(1)}, bf16[1,384,3072]{2,1,0:T(8,128)(2,1)S(1)}, u32[]{:S(2)}, u32[]{:S(2)}) %collective-permute-start.3) | collective-permute-done | bytes 2359328 | tf_op jit(solution)/shard_map/ppermute | solution.py:13
  288.2 1.4 copy-done.9
  289.6 0.0 collective-permute-start.4
  289.6 52.8 %collective-permute-done.4 = bf16[1,384,3072]{2,1,0:T(8,128)(2,1)} collective-permute-done((bf16[1,384,3072]{2,1,0:T(8,128)(2,1)S(1)}, bf16[1,384,3072]{2,1,0:T(8,128)(2,1)}, u32[]{:S(2)}, u32[]{:S(2)}) %collective-permute-start.4) | collective-permute-done | bytes 2359328 | tf_op jit(solution)/shard_map/ppermute | solution.py:13
  342.5 0.0 collective-permute-start.5
  342.5 2.4 copy.23
  344.9 34.2 %all_gather.6 = s32[1,32,10]{2,0,1:T(1,128)S(1)} all-gather(s32[1,1,10]{2,0,1:T(1,128)S(1)} %bitcast.68), channel_id=1, replica_groups=mesh['own'=32,'blk'=8] {'own'}, dimensions={1}, use_global_device_ids=true | all-gather | bytes 1320 | tf_op jit(solution)/shard_map/all_gather | solution.py:25
  379.1 0.5 broadcast.67
  379.6 0.6 reduce.3
  380.2 0.1 eq.24
  380.3 0.0 copy-start.11
  380.3 4.3 copy.18
  385.3 0.1 dynamic_slice.35
  385.4 9.3 %collective-permute-done.5 = bf16[1,384,3072]{2,1,0:T(8,128)(2,1)} collective-permute-done((bf16[1,384,3072]{2,1,0:T(8,128)(2,1)}, bf16[1,384,3072]{2,1,0:T(8,128)(2,1)}, u32[]{:S(2)}, u32[]{:S(2)}) %collective-permute-start.5) | collective-permute-done | bytes 2359328 | tf_op jit(solution)/shard_map/ppermute | solution.py:13
  394.7 0.0 collective-permute-start.6
  394.7 10.5 %fusion.20 = bf16[72,128,128]{2,0,1:T(8,128)(2,1)S(1)} fusion(bf16[320,128,128]{2,1,0:T(8,128)(2,1)} %bitcast.55, s32[320]{0:T(512)S(1)} %eq.24), kind=kOutput, calls=%fused_computation.22 | convolution fusion | flops 756177408 | bytes 12846336 | tf_op jit(solution)/shard_map/sq,sij->qij/dot_general | solution.py:31
  405.2 0.4 copy.22
  405.6 0.6 copy.33
  406.2 0.0 copy-start.2
  406.2 1.3 copy-done.1
  407.5 1.7 fusion.18
  409.2 3.3 fusion.6
  412.6 0.0 copy-start.10
  412.6 5.8 %fusion.8 = f32[3072,384]{1,0:T(8,128)} fusion(bf16[1,384,3072]{2,1,0:T(8,128)(2,1)} %collective-permute-done.4, bf16[384,3072]{1,0:T(8,128)(2,1)S(1)} %bitcast.58, s32[]{:T(128)S(6)} %select_n.73), kind=kOutput, calls=%fused_computation.10 | convolution fusion | flops 905969664 | bytes 7372804 | tf_op jit(solution)/shard_map/ac,pcb->pab/dot_general | solution.py:46
  418.4 3.9 fusion.10
  422.3 3.9 fusion.12
  426.2 3.8 fusion.14
  430.0 3.9 fusion.16
  433.9 12.0 %collective-permute-done.6 = bf16[1,384,3072]{2,1,0:T(8,128)(2,1)} collective-permute-done((bf16[1,384,3072]{2,1,0:T(8,128)(2,1)}, bf16[1,384,3072]{2,1,0:T(8,128)(2,1)}, u32[]{:S(2)}, u32[]{:S(2)}) %collective-permute-start.6) | collective-permute-done | bytes 2359328 | tf_op jit(solution)/shard_map/ppermute | solution.py:13
  445.9 13.2 %fusion.4 = bf16[1,384,3072]{1,2,0:T(8,128)(2,1)} fusion(f32[3072,384]{1,0:T(8,128)S(1)} %fusion.6, f32[3072,384]{1,0:T(8,128)} %fusion.8, f32[3072,384]{1,0:T(8,128)} %fusion.10, bf16[1,384,3072]{1,2,0:T(8,128)(2,1)} %copy.23, f32[3072,384]{1,0:T(8,128)} %fusion.12, f32[3072,384]{1,0:T(8,128)} %fusion.14, f32[3072,384]{1,0:T(8,128)S(1)} %fusion.18, ...), kind=kOutput, calls=%fused_computation.5 | convolution fusion | flops 923664384 | bytes 42776580 | tf_op jit(solution)/shard_map/ac,pcb->pab/dot_general | solution.py:46
  459.1 4.3 copy.24
  (19 shorter events, 0.0 us)
Async XLA Ops:
  6.5 388.1 %all-gather.2.cloned.1.call-start = ((), (), s32[]{:S(2)}) async-start(), calls=%async_computation | async-start | bytes 10813440 | tf_op jit(solution)/shard_map/all_gather | solution.py:24
  15.9 1.4 copy-start
  17.3 102.9 %collective-permute-start = (bf16[1,384,3072]{2,1,0:T(8,128)(2,1)S(1)}, bf16[1,384,3072]{2,1,0:T(8,128)(2,1)S(1)}, u32[]{:S(2)}, u32[]{:S(2)}) collective-permute-start(bf16[1,384,3072]{2,1,0:T(8,128)(2,1)S(1)} %mul.33), channel_id=1, source_target_pairs={{0,1},{1,2},{2,3},{3,4},{4,5},{5,6},{6,7},{7,0},{8,9},{9,10},{10,1... | collective-permute-start | bytes 7077896 | tf_op jit(solution)/shard_map/ppermute | solution.py:13
  120.2 1.4 copy-start.3
  121.6 55.5 %collective-permute-start.1 = (bf16[1,384,3072]{2,1,0:T(8,128)(2,1)S(1)}, bf16[1,384,3072]{2,1,0:T(8,128)(2,1)S(1)}, u32[]{:S(2)}, u32[]{:S(2)}) collective-permute-start(bf16[1,384,3072]{2,1,0:T(8,128)(2,1)S(1)} %collective-permute-done), channel_id=1, source_target_pairs={{0,1},{1,2},{2,3},{3,4},{4,5},{5,6},{6,7},{7,0},{8,9},{9,10},{10,1... | collective-permute-start | bytes 7077896 | tf_op jit(solution)/shard_map/ppermute | solution.py:13
  177.1 1.4 copy-start.5
  178.6 54.6 %collective-permute-start.2 = (bf16[1,384,3072]{2,1,0:T(8,128)(2,1)S(1)}, bf16[1,384,3072]{2,1,0:T(8,128)(2,1)S(1)}, u32[]{:S(2)}, u32[]{:S(2)}) collective-permute-start(bf16[1,384,3072]{2,1,0:T(8,128)(2,1)S(1)} %collective-permute-done.1), channel_id=1, source_target_pairs={{0,1},{1,2},{2,3},{3,4},{4,5},{5,6},{6,7},{7,0},{8,9},{9,10},{10,1... | collective-permute-start | bytes 7077896 | tf_op jit(solution)/shard_map/ppermute | solution.py:13
  233.1 1.4 copy-start.7
  234.6 53.6 %collective-permute-start.3 = (bf16[1,384,3072]{2,1,0:T(8,128)(2,1)S(1)}, bf16[1,384,3072]{2,1,0:T(8,128)(2,1)S(1)}, u32[]{:S(2)}, u32[]{:S(2)}) collective-permute-start(bf16[1,384,3072]{2,1,0:T(8,128)(2,1)S(1)} %collective-permute-done.2), channel_id=1, source_target_pairs={{0,1},{1,2},{2,3},{3,4},{4,5},{5,6},{6,7},{7,0},{8,9},{9,10},{10,1... | collective-permute-start | bytes 7077896 | tf_op jit(solution)/shard_map/ppermute | solution.py:13
  288.2 1.4 copy-start.9
  289.6 52.8 %collective-permute-start.4 = (bf16[1,384,3072]{2,1,0:T(8,128)(2,1)S(1)}, bf16[1,384,3072]{2,1,0:T(8,128)(2,1)}, u32[]{:S(2)}, u32[]{:S(2)}) collective-permute-start(bf16[1,384,3072]{2,1,0:T(8,128)(2,1)S(1)} %collective-permute-done.3), channel_id=1, source_target_pairs={{0,1},{1,2},{2,3},{3,4},{4,5},{5,6},{6,7},{7,0},{8,9},{9,10},{10,1... | collective-permute-start | bytes 7077896 | tf_op jit(solution)/shard_map/ppermute | solution.py:13
  342.5 52.2 %collective-permute-start.5 = (bf16[1,384,3072]{2,1,0:T(8,128)(2,1)}, bf16[1,384,3072]{2,1,0:T(8,128)(2,1)}, u32[]{:S(2)}, u32[]{:S(2)}) collective-permute-start(bf16[1,384,3072]{2,1,0:T(8,128)(2,1)} %collective-permute-done.4), channel_id=1, source_target_pairs={{0,1},{1,2},{2,3},{3,4},{4,5},{5,6},{6,7},{7,0},{8,9},{9,10},{10,1... | collective-permute-start | bytes 7077896 | tf_op jit(solution)/shard_map/ppermute | solution.py:13
  342.5 2.4 copy-start.12
  380.3 5.0 %copy-start.11 = (f32[3072]{0:T(1024)S(1)}, f32[3072]{0:T(1024)}, u32[]{:S(2)}) copy-start(f32[3072]{0:T(1024)} %param.12) | copy-start | bytes 36868
  394.7 51.2 %collective-permute-start.6 = (bf16[1,384,3072]{2,1,0:T(8,128)(2,1)}, bf16[1,384,3072]{2,1,0:T(8,128)(2,1)}, u32[]{:S(2)}, u32[]{:S(2)}) collective-permute-start(bf16[1,384,3072]{2,1,0:T(8,128)(2,1)} %collective-permute-done.5), channel_id=1, source_target_pairs={{0,1},{1,2},{2,3},{3,4},{4,5},{5,6},{6,7},{7,0},{8,9},{9,10},{10,1... | collective-permute-start | bytes 7077896 | tf_op jit(solution)/shard_map/ppermute | solution.py:13
  405.6 1.9 copy-start.1
  406.2 23.8 %copy-start.2 = (bf16[48,8,24,128]{3,1,2,0:T(8,128)(2,1)}, bf16[48,8,24,128]{3,1,2,0:T(8,128)(2,1)S(1)}, u32[]{:S(2)}) copy-start(bf16[48,8,24,128]{3,1,2,0:T(8,128)(2,1)S(1)} %copy.33) | copy-start | bytes 7077892
  412.6 5.8 %copy-start.10 = (bf16[1,384,3072]{2,1,0:T(8,128)(2,1)S(1)}, bf16[1,384,3072]{2,1,0:T(8,128)(2,1)}, u32[]{:S(2)}) copy-start(bf16[1,384,3072]{2,1,0:T(8,128)(2,1)} %copy-done.9) | copy-start | bytes 7077892
  418.4 3.9 copy-start.8
  422.2 3.9 copy-start.6
  426.2 3.8 copy-start.4
Sparse Core Ops, SparseCore 0:
  9.2 77.4 all-gather.1
where the time goes:
time: 471 us; the launch traced here: 470 us
  waiting for transfers between devices  340 us (72%)
  matrix products  50 us (11%)
  blocking collectives  34.2 us (7%)
  local copies, waits for them, and re-layouts  26.4 us (6%)
  between operations  14.2 us (3%)
    ppermute x7, waiting for transfers between devices, passed_along(): return lax.ppermute(value, axis, pairs)  339 us
    dot_general x8, matrix products, local(): jnp.einsum('ac,pcb->pab', columns, panel, preferred_element_type=jnp.floa...  39.5 us
    all_gather x1, blocking collectives, local(): labels = lax.all_gather(tile_ids, 'own', axis=1, tiled=True)  34.2 us
    unnamed x29, local copies, waits for them, and re-layouts  13.3 us
    dot_general x1, matrix products, local(): jnp.einsum('sq,sij->qij', onehot, flat_tiles, preferred_element_type=jnp....  10.5 us
  transfers between devices with their start and end apart: 8, of which 7 were waited for; matrix products, arithmetic and copies ran while one was open for 12% of the time, Pallas kernels for 0%

commit v1 on v0

v1 whole, which is shorter than its diff:
```python
import jax
import jax.numpy as jnp
from jax import lax
from jax.experimental import pallas as pl
from jax.experimental.pallas import tpu as pltpu
from jax.sharding import PartitionSpec as P

TILE = 128
NT = 24
SLOTS = 10
ROWS = 384
NV = 3072
HALF = 1536
NC = 6
CW = HALF // NC
CR = 192
ZC = 384
MESH = pl.DeviceIdType.MESH
BF = jnp.bfloat16
F32 = jnp.float32


def al(value, multiple=128):
    return pl.multiple_of(value, multiple)


def kernel(amp, mask, bare, tiles, ids, eps, pair, out,
           amps, sfull, ssend, barep, bareo, grid, gr, zr, xsend, xr, wf, op, oo, rowe,
           loc, sx, rx, sy, ry, sf, rf, sb, rb, so, ro, lo, sc, rc, sz, rz, sw, rw, sa, ra, sd, rd):
    own, blk = lax.axis_index("own"), lax.axis_index("blk")
    core, z, xl = own % 2, (own // 2) % 8, own // 16
    xh, y = blk // 4, blk % 4

    def dev(xh_=None, y_=None, xl_=None, z_=None, core_=None):
        xh_ = xh if xh_ is None else xh_
        y_ = y if y_ is None else y_
        xl_ = xl if xl_ is None else xl_
        z_ = z if z_ is None else z_
        core_ = core if core_ is None else core_
        return {"own": xl_ * 16 + z_ * 2 + core_, "blk": xh_ * 4 + y_}

    def remote(src, dst, send, recv, device):
        return pltpu.make_async_remote_copy(
            src_ref=src, dst_ref=dst, send_sem=send, recv_sem=recv,
            device_id=device, device_id_type=MESH)

    other = dev(xh_=1 - xh)
    sibling = dev(core_=1 - core)
    yn = [dev(y_=(y + 1) % 4), dev(y_=(y + 3) % 4)]
    zn = [dev(z_=(z + 1) % 8), dev(z_=(z + 7) % 8)]
    zk = [dev(z_=(z + k) % 8) for k in range(1, 8)]
    xs = [dev(xl_=1 - xl), other, dev(xh_=1 - xh, xl_=1 - xl)]

    mine, theirs = al(xh * HALF), al((1 - xh) * HALF)
    load_theirs = pltpu.make_async_copy(amp.at[:, pl.ds(theirs, HALF)], amps.at[:, pl.ds(0, HALF)], loc.at[0])
    load_mine = pltpu.make_async_copy(amp.at[:, pl.ds(mine, HALF)], amps.at[:, pl.ds(HALF, HALF)], loc.at[1])
    load_bare = pltpu.make_async_copy(bare.at[:, pl.ds(mine, HALF)], bareo, loc.at[2])
    load_theirs.start()
    load_mine.start()
    load_bare.start()

    barrier = pltpu.get_barrier_semaphore()
    peers = [sibling] + yn + zk + xs
    for peer in peers:
        pl.semaphore_signal(barrier, inc=1, device_id=peer, device_id_type=MESH)
    pl.semaphore_wait(barrier, len(peers))

    def rows_of(xh_, y_):
        return pl.ds(al((xh_ * 4 + y_) * ROWS), ROWS)

    def cols(n):
        return pl.ds(al(n * CW), CW)

    def x_copy(n):
        return remote(ssend.at[:, cols(n)], sfull.at[rows_of(xh, y), cols(n)], sx.at[n], rx.at[n], other)

    def y_copy(part, d, n):
        where = sfull.at[rows_of(xh if part == 0 else 1 - xh, y), cols(n)]
        return remote(where, where, sy.at[part, d, n], ry.at[part, d, n], yn[d])

    def f_copy(d, n):
        where = sfull.at[rows_of(xh if d == 0 else 1 - xh, (y + 3) % 4 if d == 0 else (y + 1) % 4), cols(n)]
        return remote(where, where, sf.at[d, n], rf.at[d, n], yn[d])

    def b_copy(n):
        return remote(bare.at[:, pl.ds(al(theirs + n * CW), CW)], barep.at[:, cols(n)], sb.at[n], rb.at[n], other)

    def o_copy(n):
        return remote(op.at[:, cols(n)], out.at[:, pl.ds(al(mine + n * CW), CW)], so.at[n], ro.at[n], other)

    def own_out(n):
        return pltpu.make_async_copy(oo.at[:, cols(n)], out.at[:, pl.ds(al(mine + n * CW), CW)], lo.at[n])

    load_theirs.wait()
    load_mine.wait()

    def screen(n, _):
        for side in range(2):
            first = (1 - xh) if side == 0 else xh
            for r in range(3):
                for c in range(CW // TILE):
                    keep = mask[r, first * (NT // 2) + n * (CW // TILE) + c]
                    here = al(n * CW + c * TILE)
                    tile = amps[r * TILE:(r + 1) * TILE, pl.ds(al(side * HALF + here), TILE)]
                    tile = jnp.where(keep > 0, tile, jnp.zeros_like(tile))
                    if side == 0:
                        ssend[r * TILE:(r + 1) * TILE, pl.ds(here, TILE)] = tile
                    else:
                        sfull[pl.ds(al(blk * ROWS + r * TILE), TILE), pl.ds(here, TILE)] = tile
            if side == 0:
                x_copy(n).start()
        y_copy(0, 0, n).start()
        y_copy(0, 1, n).start()
        return 0

    lax.fori_loop(0, NC, screen, 0)

    def place(q, _):
        index, found = 0, 0
        for s in range(SLOTS):
            hit = ids[s] == q
            index = jnp.where(hit, s, index)
            found = jnp.where(hit, 1, found)
        tile = tiles[index]
        grid[pl.ds(al(q // NT * TILE), TILE), pl.ds(al(q % NT * TILE), TILE)] = jnp.where(
            found > 0, tile, jnp.zeros_like(tile))
        return 0

    lax.fori_loop(0, 3 * NT, place, 0)
    half_rows = pl.ds(al(core * CR, 16), CR)
    c_copy = remote(grid.at[pl.ds(al((1 - core) * CR, 16), CR), :], gr, sc, rc, sibling)
    c_copy.start()

    for side in range(2):
        for r in range(3):
            line = eps[pl.ds((side * 4 + y) * 3 + r, 1), :]
            rowe[side, r] = jnp.transpose(jnp.broadcast_to(line, (TILE, TILE)))

    c_copy.wait_recv()

    def add_core(k, _):
        at = pl.ds(al(k * ZC), ZC)
        grid[half_rows, at] = grid[half_rows, at] + gr[:, at]
        return 0

    lax.fori_loop(0, 8, add_core, 0)

    def z_copy(k):
        return remote(grid.at[half_rows, pl.ds(al((z + k) % 8 * ZC), ZC)], zr.at[k - 1], sz.at[k - 1], rz.at[k - 1], zk[k - 1])

    for k in (1, 7, 2, 6, 3, 5, 4):
        z_copy(k).start()

    def spread(n, _):
        x_copy(n).wait_recv()
        y_copy(1, 0, n).start()
        y_copy(1, 1, n).start()
        y_copy(0, 0, n).wait_recv()
        f_copy(0, n).start()
        return 0

    lax.fori_loop(0, NC, spread, 0)
    for n in range(2):
        b_copy(n).start()

    for k in range(1, 8):
        z_copy(k).wait_recv()
    total = grid[half_rows, pl.ds(al(z * ZC), ZC)]
    for k in range(7):
        total = total + zr[k]
    xsend[...] = total
    w_copies = [remote(xsend, xr.at[k], sw.at[k], rw.at[k], xs[k]) for k in range(3)]
    for copy in w_copies:
        copy.start()
    for n in range(2, NC):
        b_copy(n).start()

    def piece(z_, side=None):
        first = slice(None) if side is None else side
        return wf.at[first, half_rows, pl.ds(al(z_ * ZC), ZC)]

    def a_copy(d, s):
        z_ = (z + 8 - s) % 8 if d == 0 else (z + s) % 8
        where = piece(z_, d if s == 3 else None)
        return remote(where, where, sa.at[d, s], ra.at[d, s], zn[d])

    def d_copy(d, s):
        z_ = (z + 8 - s) % 8 if d == 0 else (z + s) % 8
        where = piece(z_, d if s == 4 else None)
        at = 4 * d + s
        return remote(where, where, sd.at[at], rd.at[at], sibling)

    for copy in w_copies:
        copy.wait_recv()
    here = pl.ds(al(z * ZC), ZC)
    wf[xh, half_rows, here] = xsend[...] + xr[0]
    wf[1 - xh, half_rows, here] = xr[1] + xr[2]
    a_copy(0, 0).start()
    a_copy(1, 0).start()
    d_copy(0, 0).start()

    def partner_on(n):
        y_copy(1, 1, n).wait_recv()
        f_copy(1, n).start()

    for s in range(1, 4):
        partner_on(2 * s - 2)
        partner_on(2 * s - 1)
        for d in range(2):
            a_copy(d, s - 1).wait_recv()
            a_copy(d, s).start()
            d_copy(d, s).start()
    for d in range(2):
        a_copy(d, 3).wait_recv()
        d_copy(d, 4).start()
    load_bare.wait()
    d_copy(0, 0).wait_recv()
    for s in range(1, 5):
        for d in range(2):
            d_copy(d, s).wait_recv()

    energy = pair[0]

    def work(n, _):
        y_copy(0, 1, n).wait_recv()
        y_copy(1, 0, n).wait_recv()
        f_copy(0, n).wait_recv()
        f_copy(1, n).wait_recv()
        b_copy(n).wait_recv()
        for which in range(2):
            side = (1 - xh) if which == 0 else xh
            source, target = (barep, op) if which == 0 else (bareo, oo)
            total = jnp.dot(wf[side], sfull[:, cols(n)], preferred_element_type=F32)
            for r in range(3):
                for c in range(CW // TILE):
                    at = pl.ds(al(n * CW + c * TILE), TILE)
                    line = eps[pl.ds(xh * (NT // 2) + n * (CW // TILE) + c, 1), :]
                    denom = (rowe[side, r] + line) - energy
                    value = source[r * TILE:(r + 1) * TILE, at].astype(F32) + total[r * TILE:(r + 1) * TILE, c * TILE:(c + 1) * TILE]
                    target[r * TILE:(r + 1) * TILE, at] = (value / denom).astype(BF)
            if which == 0:
                o_copy(n).start()
            else:
                own_out(n).start()
        return 0

    lax.fori_loop(0, NC, work, 0)

    def drain(n, _):
        own_out(n).wait()
        x_copy(n).wait_send()
        b_copy(n).wait_send()
        for d in range(2):
            y_copy(0, d, n).wait_send()
            y_copy(1, d, n).wait_send()
            f_copy(d, n).wait_send()
        o_copy(n).wait_send()
        o_copy(n).wait_recv()
        return 0

    lax.fori_loop(0, NC, drain, 0)
    c_copy.wait_send()
    for k in range(1, 8):
        z_copy(k).wait_send()
    for copy in w_copies:
        copy.wait_send()
    d_copy(0, 0).wait_send()
    for d in range(2):
        for s in range(4):
            a_copy(d, s).wait_send()
            d_copy(d, s + 1).wait_send()


def apply_mask(mask, raw, out):
    for r in range(3):
        for c in range(NT):
            at = (slice(r * TILE, (r + 1) * TILE), slice(c * TILE, (c + 1) * TILE))
            tile = raw[at]
            out[at] = jnp.where(mask[r, c] > 0, tile, jnp.zeros_like(tile))


def local(amplitudes, amp_mask, bare_ints, int_tiles, tile_ids, eps_virt, eps_pair):
    dma = pltpu.SemaphoreType.DMA
    vmem = pltpu.VMEM
    mask = amp_mask.reshape(3, NT)
    anywhere = pl.BlockSpec(memory_space=pl.ANY)
    smem = pl.BlockSpec(memory_space=pltpu.SMEM)
    inside = pl.BlockSpec(memory_space=pltpu.VMEM)
    pairs_of = [dma((NC,)), dma((NC,)), dma((2, 2, NC)), dma((2, 2, NC)), dma((2, NC)), dma((2, NC)),
                dma((NC,)), dma((NC,)), dma((NC,)), dma((NC,)), dma((NC,)),
                dma, dma, dma((7,)), dma((7,)), dma((3,)), dma((3,)),
                dma((2, 4)), dma((2, 4)), dma((9,)), dma((9,))]
    raw = pl.pallas_call(
        kernel,
        out_shape=jax.ShapeDtypeStruct((ROWS, NV), BF),
        in_specs=[anywhere, smem, anywhere, inside, smem, inside, smem],
        out_specs=anywhere,
        scratch_shapes=[
            vmem((ROWS, NV), BF), vmem((NV, HALF), BF), vmem((ROWS, HALF), BF), vmem((ROWS, HALF), BF),
            vmem((ROWS, HALF), BF), vmem((ROWS, NV), BF), vmem((CR, NV), BF), vmem((7, CR, ZC), BF),
            vmem((CR, ZC), BF), vmem((3, CR, ZC), BF), vmem((2, ROWS, NV), BF), vmem((ROWS, HALF), BF),
            vmem((ROWS, HALF), BF), vmem((2, 3, TILE, TILE), F32),
            dma((3,)), *pairs_of,
        ],
        compiler_params=pltpu.CompilerParams(
            collective_id=0, has_side_effects=True, vmem_limit_bytes=56 * 1024 * 1024),
        name="cycle",
    )(amplitudes.reshape(ROWS, NV), mask, bare_ints.reshape(ROWS, NV), int_tiles.reshape(SLOTS, TILE, TILE),
      tile_ids.reshape(SLOTS), eps_virt.reshape(NT, TILE), eps_pair)
    final = pl.pallas_call(
        apply_mask,
        out_shape=jax.ShapeDtypeStruct((ROWS, NV), BF),
        in_specs=[smem, inside],
        out_specs=inside,
        name="screen",
    )(mask, raw)
    return final.reshape(1, ROWS, NV)


def solution(mesh):
    in_specs = (
        P("own", "blk", None),
        P("own", "blk", None),
        P("own", "blk", None),
        P("blk", "own", None, None, None),
        P("blk", "own", None),
        P(),
        P("own"),
    )
    return jax.shard_map(local, mesh=mesh, in_specs=in_specs, out_specs=P("own", "blk", None), check_vma=False)
```

time: 471 us -> 123 us (0.26)
  waiting for transfers between devices: 340 us -> 0 us
  Pallas kernels: 0 us -> 119 us
  matrix products: 50 us -> 0 us
  blocking collectives: 34.2 us -> 0 us
  local copies, waits for them, and re-layouts: 26.4 us -> 1.27 us
  between operations: 14.2 us -> 0.66 us
    ppermute x7 -> x0, waiting for transfers between devices: 339 us -> none  [passed_along(): return lax.ppermute(value, axis, pairs)]
    pallas_call x0 -> x2, Pallas kernels: none -> 119 us  [the longest x1 115 us: local(): pl.pallas_call(kernel, out_shape=jax.ShapeDtypeStruct((ROWS, NV), BF), in...]
    dot_general x9 -> x0, matrix products: 50 us -> none  [the longest x8 39.5 us: local(): jnp.einsum('ac,pcb->pab', columns, panel, preferred_element_type=jnp.floa...]
    all_gather x1 -> x0, blocking collectives: 34.2 us -> none  [local(): labels = lax.all_gather(tile_ids, 'own', axis=1, tiled=True)]
    unnamed x29 -> x1, local copies, waits for them, and re-layouts: 13.3 us -> 1.27 us
    broadcast_in_dim x3 -> x0, local copies, waits for them, and re-layouts: 7.83 us -> none  [local(): jnp.broadcast_to(amp_mask.astype(jnp.bfloat16)[:, :, None, :, None], (pai...]
  transfers between devices with their start and end apart: 8 -> 0, of which waited for: 7 -> 0; matrix products, arithmetic and copies ran while one was open for 12% -> 0% of each run, Pallas kernels for 0% -> 0%
where the time goes in v1:
time: 123 us; the launch traced here: 121 us
  Pallas kernels  119 us (97%)
  local copies, waits for them, and re-layouts  1.27 us (1%)
    pallas_call x1, Pallas kernels, local(): pl.pallas_call(kernel, out_shape=jax.ShapeDtypeStruct((ROWS, NV), BF), in...  115 us
    pallas_call x1, Pallas kernels, local(): pl.pallas_call(apply_mask, out_shape=jax.ShapeDtypeStruct((ROWS, NV), BF)...  3.74 us

profile of v1, /device:TPU:2, one launch (start us, length us, event | category | flops | bytes accessed | tf_op | source)
XLA Modules:
  0.0 121.0 jit_solution(5558230266540014639)
XLA Ops:
  0.7 1.3 %copy.10 = s32[1,3,24]{2,1,0:T(4,128)} copy(s32[1,3,24]{2,0,1:T(1,128)} %param.8) | data formatting | bytes 576
  1.9 115.3 %cycle.1.raw = bf16[384,3072]{1,0:T(8,128)(2,1)} custom-call(bf16[384,3072]{1,0:T(8,128)(2,1)} %bitcast.9, s32[3,24]{1,0:T(4,128)} %bitcast.12, bf16[384,3072]{1,0:T(8,128)(2,1)} %bitcast.10, bf16[10,128,128]{2,1,0:T(8,128)(2,1)} %bitcast.11, s32[10]{0:T(128)} %bitcast.15, f32[24,128]{1,0:T(8,128)} %bitcast.14, f32[1]{0:T(128)S(6)} %copy.11.pair), custom_call_target="tpu_custom_call" | custom-call | tf_op jit(solution)/shard_map/cycle/pallas_call | solution.py:293
  117.3 3.7 %screen.1 = bf16[384,3072]{1,0:T(8,128)(2,1)} custom-call(s32[3,24]{1,0:T(4,128)} %bitcast.13, bf16[384,3072]{1,0:T(8,128)(2,1)} %cycle.1.raw), custom_call_target="tpu_custom_call" | custom-call | tf_op jit(solution)/shard_map/screen/pallas_call | solution.py:310

commit v2 on v0

v2 whole, which is shorter than its diff:
```python
import jax
import jax.numpy as jnp
from jax import lax
from jax.experimental import pallas as pl
from jax.experimental.pallas import tpu as pltpu
from jax.sharding import PartitionSpec as P

TILE = 128
NT = 24
SLOTS = 10
ROWS = 384
NV = 3072
HALF = 1536
QR = 32
ZC = 384
STARTS = (0, 256, 512, 768, 1024, 1280, 1408)
WIDTHS = (256, 256, 256, 256, 256, 128, 128)
NC = len(STARTS)
WIDE = 256
MESH = pl.DeviceIdType.MESH
BF = jnp.bfloat16
F32 = jnp.float32


def al(value, multiple=128):
    return pl.multiple_of(value, multiple)


def kernel(amp, mask, bare, tiles, ids, eps, pair, out,
           amps, sfull, ssend, barep, bareo, inv, tr, grid, zr, xsend, xr, wf, op, oo, rowe, mv,
           loc, sx, rx, sy, ry, sf, rf, sb, rb, so, ro, lo, sm, rm, si, ri, st, rt, sz, rz, sw, rw, sa, ra, sd, rd):
    own, blk = lax.axis_index("own"), lax.axis_index("blk")
    core, z, xl = own % 2, (own // 2) % 8, own // 16
    xh, y = blk // 4, blk % 4

    def dev(xh_=None, y_=None, xl_=None, z_=None, core_=None):
        xh_ = xh if xh_ is None else xh_
        y_ = y if y_ is None else y_
        xl_ = xl if xl_ is None else xl_
        z_ = z if z_ is None else z_
        core_ = core if core_ is None else core_
        return {"own": xl_ * 16 + z_ * 2 + core_, "blk": xh_ * 4 + y_}

    def remote(src, dst, send, recv, device):
        return pltpu.make_async_remote_copy(
            src_ref=src, dst_ref=dst, send_sem=send, recv_sem=recv,
            device_id=device, device_id_type=MESH)

    other = dev(xh_=1 - xh)
    sibling = dev(core_=1 - core)
    yn = [dev(y_=(y + 1) % 4), dev(y_=(y + 3) % 4)]
    zk = [dev(z_=(z + k) % 8) for k in range(1, 8)]
    zn = [zk[0], zk[6]]
    xs = [dev(xl_=1 - xl), other, dev(xh_=1 - xh, xl_=1 - xl)]
    quad = [sibling, dev(xl_=1 - xl), dev(xl_=1 - xl, core_=1 - core)]
    quarter = core * 2 + xl
    quarters = [(1 - core) * 2 + xl, core * 2 + 1 - xl, (1 - core) * 2 + 1 - xl]

    mine, theirs = al(xh * HALF), al((1 - xh) * HALF)
    load_theirs = pltpu.make_async_copy(amp.at[:, pl.ds(theirs, HALF)], amps.at[:, pl.ds(0, HALF)], loc.at[0])
    load_mine = pltpu.make_async_copy(amp.at[:, pl.ds(mine, HALF)], amps.at[:, pl.ds(HALF, HALF)], loc.at[1])
    load_bare = pltpu.make_async_copy(bare.at[:, pl.ds(mine, HALF)], bareo, loc.at[2])
    load_theirs.start()
    load_mine.start()
    load_bare.start()

    barrier = pltpu.get_barrier_semaphore()
    peers = yn + zk + xs + [sibling, quad[2]]
    for peer in peers:
        pl.semaphore_signal(barrier, inc=1, device_id=peer, device_id_type=MESH)

    def invert(q, _):
        slot = SLOTS
        for s in range(SLOTS):
            slot = jnp.where(ids[s] == q, s, slot)
        inv[0, q] = slot
        return 0

    lax.fori_loop(0, 3 * NT, invert, 0)
    pl.semaphore_wait(barrier, len(peers))

    def rows_of(xh_, y_):
        return pl.ds(al((xh_ * 4 + y_) * ROWS), ROWS)

    def part(n, base=0):
        if isinstance(n, int):
            return pl.ds(al(base + STARTS[n]), WIDTHS[n])
        return pl.ds(al(base + n * WIDE), WIDE)

    def x_copy(n):
        return remote(ssend.at[:, part(n)], sfull.at[rows_of(xh, y), part(n)], sx.at[n], rx.at[n], other)

    def y_copy(b, d, n):
        where = sfull.at[rows_of(xh if b == 0 else 1 - xh, y), part(n)]
        return remote(where, where, sy.at[b, d, n], ry.at[b, d, n], yn[d])

    def f_copy(d, n):
        where = sfull.at[rows_of(xh if d == 0 else 1 - xh, (y + 3) % 4 if d == 0 else (y + 1) % 4), part(n)]
        return remote(where, where, sf.at[d, n], rf.at[d, n], yn[d])

    def b_copy(n):
        return remote(bare.at[:, part(n, theirs)], barep.at[:, part(n)], sb.at[n], rb.at[n], other)

    def o_copy(n):
        return remote(op.at[:, part(n)], out.at[:, part(n, mine)], so.at[n], ro.at[n], other)

    def own_out(n):
        at = n * WIDE
        return pltpu.make_async_copy(oo.at[:, pl.ds(al(at), WIDE)], out.at[:, pl.ds(al(mine + at), WIDE)], lo.at[n])

    def t_copy(j):
        return remote(tiles.at[:, pl.ds(al(quarters[j] * QR, QR), QR), :], tr.at[j + 1, pl.ds(0, SLOTS)], st.at[j], rt.at[j], quad[j])

    def i_copy(j):
        return remote(inv.at[0], inv.at[j + 1], si.at[j], ri.at[j], quad[j])

    for j in range(3):
        t_copy(j).start()
        i_copy(j).start()

    def screen(n):
        count = WIDTHS[n] // TILE
        for side in range(2):
            first = (1 - xh) if side == 0 else xh
            for c in range(count):
                here = STARTS[n] + c * TILE
                for r in range(3):
                    keep = mask[r, 0, first * (NT // 2) + here // TILE]
                    tile = amps[r * TILE:(r + 1) * TILE, side * HALF + here:side * HALF + here + TILE]
                    tile = jnp.where(keep > 0, tile, jnp.zeros_like(tile))
                    if side == 0:
                        ssend[r * TILE:(r + 1) * TILE, here:here + TILE] = tile
                    else:
                        sfull[pl.ds(al(blk * ROWS + r * TILE), TILE), here:here + TILE] = tile
            if side == 0:
                x_copy(n).start()
        y_copy(0, 0, n).start()
        y_copy(0, 1, n).start()

    load_theirs.wait()
    load_mine.wait()
    screen(0)
    screen(1)

    for s in range(SLOTS):
        tr[0, s] = tiles[s, pl.ds(al(quarter * QR, QR), QR), :]
    for j in range(4):
        tr[j, SLOTS] = jnp.zeros((QR, TILE), BF)
    for j in range(3):
        t_copy(j).wait_recv()
        i_copy(j).wait_recv()

    def place(q, _):
        tile = tr[0, inv[0, q]]
        for j in range(1, 4):
            tile = tile + tr[j, inv[j, q]]
        grid[pl.ds(al(q // NT * QR, QR), QR), pl.ds(al(q % NT * TILE), TILE)] = tile
        return 0

    lax.fori_loop(0, 3 * NT, place, 0)
    here = pl.ds(al(z * ZC), ZC)

    def z_copy(k):
        return remote(grid.at[:, pl.ds(al((z + k) % 8 * ZC), ZC)], zr.at[k - 1], sz.at[k - 1], rz.at[k - 1], zk[k - 1])

    for k in (4, 3, 5, 2, 6, 1, 7):
        z_copy(k).start()

    for n in range(2, NC):
        screen(n)

    def spread_mask(c, _):
        for r in range(3):
            mv[1, r, pl.ds(c, 1), :] = jnp.full((1, TILE), mask[r, 0, c].astype(F32))
        return 0

    lax.fori_loop(0, NT, spread_mask, 0)
    m_copy = remote(mv.at[1], mv.at[0], sm, rm, other)
    m_copy.start()

    for side in range(2):
        for r in range(3):
            line = eps[pl.ds((side * 4 + y) * 3 + r, 1), :]
            rowe[side, r] = jnp.transpose(jnp.broadcast_to(line, (TILE, TILE)))

    def spread(n):
        x_copy(n).wait_recv()
        y_copy(1, 0, n).start()
        y_copy(1, 1, n).start()
        y_copy(0, 0, n).wait_recv()
        f_copy(0, n).start()

    def partner_on(n):
        y_copy(1, 1, n).wait_recv()
        f_copy(1, n).start()

    def w_copy(k):
        return remote(xsend, xr.at[k], sw.at[k], rw.at[k], xs[k])

    def reduce_z():
        for k in range(1, 8):
            z_copy(k).wait_recv()
        total = grid[:, here]
        for k in range(7):
            total = total + zr[k]
        xsend[...] = total
        for k in range(3):
            w_copy(k).start()

    def reduce_x():
        for k in range(3):
            w_copy(k).wait_recv()
        for r in range(3):
            rows = slice(r * QR, (r + 1) * QR)
            wf[xh, r, quarter, :, here] = xsend[rows, :]
            wf[xh, r, quarters[1], :, here] = xr[0, rows, :]
            wf[1 - xh, r, quarter, :, here] = xr[1, rows, :]
            wf[1 - xh, r, quarters[1], :, here] = xr[2, rows, :]

    def piece(g, z_, q=None):
        which = pl.ds(core * 2, 2) if q is None else pl.ds(core * 2 + q, 1)
        return wf.at[1 - xh if g == 0 else xh, :, which, :, pl.ds(al(z_ * ZC), ZC)]

    def from_z(d, s):
        return (z + 8 - s) % 8 if d == 0 else (z + s) % 8

    def a_copy(g, d, s):
        where = piece(g, from_z(d, s), d if s == 3 else None)
        return remote(where, where, sa.at[g, d, s], ra.at[g, d, s], zn[d])

    def d_copy(g, d, s):
        where = piece(g, from_z(d, s), d if s == 4 else None)
        return remote(where, where, sd.at[g, 4 * d + s], rd.at[g, 4 * d + s], sibling)

    def begin(g):
        a_copy(g, 0, 0).start()
        a_copy(g, 1, 0).start()
        d_copy(g, 0, 0).start()

    def onward(g, s):
        for d in range(2):
            a_copy(g, d, s - 1).wait_recv()
            if s < 4:
                a_copy(g, d, s).start()
            d_copy(g, d, s).start()

    def gathered(g):
        d_copy(g, 0, 0).wait_recv()
        for s in range(1, 5):
            for d in range(2):
                d_copy(g, d, s).wait_recv()

    for n in range(4):
        spread(n)
    reduce_z()
    spread(4)
    spread(5)
    spread(6)
    reduce_x()
    begin(0)
    begin(1)
    for n in range(NC):
        b_copy(n).start()
    onward(0, 1)
    onward(1, 1)
    onward(0, 2)
    partner_on(0)
    onward(1, 2)
    partner_on(1)
    onward(0, 3)
    partner_on(2)
    onward(1, 3)
    onward(0, 4)
    partner_on(3)
    onward(1, 4)
    partner_on(4)
    partner_on(5)
    partner_on(6)
    load_bare.wait()
    m_copy.wait_recv()
    gathered(0)
    gathered(1)

    energy = pair[0]

    def rows_done(start, width, which):
        side = (1 - xh) if which == 0 else xh
        source, target = (barep, op) if which == 0 else (bareo, oo)
        total = jnp.dot(wf[side].reshape(ROWS, NV), sfull[:, pl.ds(al(start), width)], preferred_element_type=F32)
        for c in range(width // TILE):
            at = pl.ds(al(start + c * TILE), TILE)
            column = xh * (NT // 2) + start // TILE + c
            line = eps[pl.ds(column, 1), :]
            for r in range(3):
                rows = slice(r * TILE, (r + 1) * TILE)
                denom = (rowe[side, r] + line) - energy
                value = source[rows, at].astype(F32) + total[rows, c * TILE:(c + 1) * TILE]
                target[rows, at] = (value / denom * mv[which, r, pl.ds(column, 1), :]).astype(BF)

    def theirs_done(n, start, width):
        y_copy(0, 1, n).wait_recv()
        y_copy(1, 0, n).wait_recv()
        f_copy(0, n).wait_recv()
        f_copy(1, n).wait_recv()
        b_copy(n).wait_recv()
        rows_done(start, width, 0)
        o_copy(n).start()

    def mine_done(n):
        rows_done(n * WIDE, WIDE, 1)
        own_out(n).start()

    theirs_done(0, 0, WIDE)

    def work(n, _):
        theirs_done(n, n * WIDE, WIDE)
        mine_done(n - 1)
        return 0

    lax.fori_loop(1, 5, work, 0)
    theirs_done(5, STARTS[5], WIDTHS[5])
    mine_done(4)
    theirs_done(6, STARTS[6], WIDTHS[6])
    mine_done(5)

    for n in range(6):
        own_out(n).wait()
    for j in range(3):
        t_copy(j).wait_send()
        i_copy(j).wait_send()
    m_copy.wait_send()
    for n in range(NC):
        x_copy(n).wait_send()
        b_copy(n).wait_send()
        for d in range(2):
            y_copy(0, d, n).wait_send()
            y_copy(1, d, n).wait_send()
            f_copy(d, n).wait_send()
    for k in range(1, 8):
        z_copy(k).wait_send()
    for k in range(3):
        w_copy(k).wait_send()
    for g in range(2):
        d_copy(g, 0, 0).wait_send()
        for d in range(2):
            for t in range(4):
                a_copy(g, d, t).wait_send()
                d_copy(g, d, t + 1).wait_send()
    for n in range(NC):
        o_copy(n).wait_send()
        o_copy(n).wait_recv()


def local(amplitudes, amp_mask, bare_ints, int_tiles, tile_ids, eps_virt, eps_pair):
    dma = pltpu.SemaphoreType.DMA
    vmem = pltpu.VMEM
    anywhere = pl.BlockSpec(memory_space=pl.ANY)
    smem = pl.BlockSpec(memory_space=pltpu.SMEM)
    inside = pl.BlockSpec(memory_space=pltpu.VMEM)
    sizes = [(NC,), (2, 2, NC), (2, NC), (NC,), (NC,)]
    sems = [dma(size) for size in sizes for _ in range(2)] + [dma((6,)), dma, dma]
    sems += [dma(size) for size in [(3,), (3,), (7,), (3,), (2, 2, 4), (2, 9)] for _ in range(2)]
    result = pl.pallas_call(
        kernel,
        out_shape=jax.ShapeDtypeStruct((ROWS, NV), BF),
        in_specs=[anywhere, smem, anywhere, inside, smem, inside, smem],
        out_specs=anywhere,
        scratch_shapes=[
            vmem((ROWS, NV), BF), vmem((NV, HALF), BF), vmem((ROWS, HALF), BF), vmem((ROWS, HALF), BF),
            vmem((ROWS, HALF), BF), pltpu.SMEM((4, TILE), jnp.int32), vmem((4, SLOTS + 1, QR, TILE), BF),
            vmem((3 * QR, NV), BF), vmem((7, 3 * QR, ZC), BF), vmem((3 * QR, ZC), BF), vmem((3, 3 * QR, ZC), BF),
            vmem((2, 3, 4, QR, NV), BF), vmem((ROWS, HALF), BF), vmem((ROWS, HALF), BF),
            vmem((2, 3, TILE, TILE), F32), vmem((2, 3, NT, TILE), F32),
            dma((3,)), *sems,
        ],
        compiler_params=pltpu.CompilerParams(
            collective_id=0, has_side_effects=True, vmem_limit_bytes=56 * 1024 * 1024),
        name="cycle",
    )(amplitudes.reshape(ROWS, NV), amp_mask.reshape(3, 1, NT), bare_ints.reshape(ROWS, NV),
      int_tiles.reshape(SLOTS, TILE, TILE), tile_ids.reshape(SLOTS), eps_virt.reshape(NT, TILE), eps_pair)
    return result.reshape(1, ROWS, NV)


def solution(mesh):
    in_specs = (
        P("own", "blk", None),
        P("own", "blk", None),
        P("own", "blk", None),
        P("blk", "own", None, None, None),
        P("blk", "own", None),
        P(),
        P("own"),
    )
    return jax.shard_map(local, mesh=mesh, in_specs=in_specs, out_specs=P("own", "blk", None), check_vma=False)
```

time: 471 us -> 105 us (0.22)
  waiting for transfers between devices: 340 us -> 0 us
  Pallas kernels: 0 us -> 99.6 us
  matrix products: 50 us -> 0 us
  blocking collectives: 34.2 us -> 0 us
  local copies, waits for them, and re-layouts: 26.4 us -> 3.22 us
  between operations: 14.2 us -> 0.66 us
    ppermute x7 -> x0, waiting for transfers between devices: 339 us -> none  [passed_along(): return lax.ppermute(value, axis, pairs)]
    pallas_call x0 -> x1, Pallas kernels: none -> 99.6 us  [local(): pl.pallas_call(kernel, out_shape=jax.ShapeDtypeStruct((ROWS, NV), BF), in...]
    dot_general x9 -> x0, matrix products: 50 us -> none  [the longest x8 39.5 us: local(): jnp.einsum('ac,pcb->pab', columns, panel, preferred_element_type=jnp.floa...]
    all_gather x1 -> x0, blocking collectives: 34.2 us -> none  [local(): labels = lax.all_gather(tile_ids, 'own', axis=1, tiled=True)]
    unnamed x29 -> x1, local copies, waits for them, and re-layouts: 13.3 us -> 3.22 us
    broadcast_in_dim x3 -> x0, local copies, waits for them, and re-layouts: 7.83 us -> none  [local(): jnp.broadcast_to(amp_mask.astype(jnp.bfloat16)[:, :, None, :, None], (pai...]
  transfers between devices with their start and end apart: 8 -> 0, of which waited for: 7 -> 0; matrix products, arithmetic and copies ran while one was open for 12% -> 0% of each run, Pallas kernels for 0% -> 0%
where the time goes in v2:
time: 105 us; the launch traced here: 103 us
  Pallas kernels  99.6 us (95%)
  local copies, waits for them, and re-layouts  3.22 us (3%)
    pallas_call x1, Pallas kernels, local(): pl.pallas_call(kernel, out_shape=jax.ShapeDtypeStruct((ROWS, NV), BF), in...  99.6 us
    unnamed x1, local copies, waits for them, and re-layouts  3.22 us

profile of v2, /device:TPU:2, one launch (start us, length us, event | category | flops | bytes accessed | tf_op | source)
XLA Modules:
  0.0 103.4 jit_solution(13223140434069202182)
XLA Ops:
  0.7 99.6 %cycle.1 = bf16[384,3072]{1,0:T(8,128)(2,1)} custom-call(bf16[384,3072]{1,0:T(8,128)(2,1)} %bitcast.8, s32[3,1,24]{2,1,0:T(1,128)} %bitcast.12, bf16[384,3072]{1,0:T(8,128)(2,1)} %bitcast.9, bf16[10,128,128]{2,1,0:T(8,128)(2,1)} %bitcast.10, s32[10]{0:T(128)} %bitcast.13, f32[24,128]{1,0:T(8,128)} %bitcast.11, f32[1]{0:T(128)S(6)} %copy.9.pair), custom_call_target="tpu_custom_call" | custom-call | tf_op jit(solution)/shard_map/cycle/pallas_call | solution.py:363
  100.2 3.2 %copy.10 = bf16[1,384,3072]{2,1,0:T(8,128)(2,1)} copy(bf16[1,384,3072]{2,1,0:T(8,128)(2,1)} %bitcast.7) | data formatting | bytes 4718592

commit v3 on v2

--- a/solution.py
+++ b/solution.py
@@ -27,8 +27,8 @@
 
 
 def kernel(amp, mask, bare, tiles, ids, eps, pair, out,
-           amps, sfull, ssend, barep, bareo, inv, tr, grid, zr, xsend, xr, wf, op, oo, rowe, mv,
-           loc, sx, rx, sy, ry, sf, rf, sb, rb, so, ro, lo, sm, rm, si, ri, st, rt, sz, rz, sw, rw, sa, ra, sd, rd):
+           amps, sfull, ssend, barep, bareo, inv, tr, grid, zr, xsend, xr, wf, op, rowe, mv,
+           loc, sx, rx, sy, ry, sf, rf, sb, rb, so, ro, sm, rm, si, ri, st, rt, sz, rz, sw, rw, sa, ra, sd, rd):
     own, blk = lax.axis_index("own"), lax.axis_index("blk")
     core, z, xl = own % 2, (own // 2) % 8, own // 16
     xh, y = blk // 4, blk % 4
@@ -104,10 +104,6 @@
     def o_copy(n):
         return remote(op.at[:, part(n)], out.at[:, part(n, mine)], so.at[n], ro.at[n], other)
 
-    def own_out(n):
-        at = n * WIDE
-        return pltpu.make_async_copy(oo.at[:, pl.ds(al(at), WIDE)], out.at[:, pl.ds(al(mine + at), WIDE)], lo.at[n])
-
     def t_copy(j):
         return remote(tiles.at[:, pl.ds(al(quarters[j] * QR, QR), QR), :], tr.at[j + 1, pl.ds(0, SLOTS)], st.at[j], rt.at[j], quad[j])
 
@@ -118,7 +114,7 @@
         t_copy(j).start()
         i_copy(j).start()
 
-    def screen(n):
+    def screen(n, send=True):
         count = WIDTHS[n] // TILE
         for side in range(2):
             first = (1 - xh) if side == 0 else xh
@@ -132,15 +128,16 @@
                         ssend[r * TILE:(r + 1) * TILE, here:here + TILE] = tile
                     else:
                         sfull[pl.ds(al(blk * ROWS + r * TILE), TILE), here:here + TILE] = tile
-            if side == 0:
+            if side == 0 and send:
                 x_copy(n).start()
         y_copy(0, 0, n).start()
         y_copy(0, 1, n).start()
 
     load_theirs.wait()
     load_mine.wait()
-    screen(0)
-    screen(1)
+    for n in range(4):
+        screen(n)
+    b_copy(0).start()
 
     for s in range(SLOTS):
         tr[0, s] = tiles[s, pl.ds(al(quarter * QR, QR), QR), :]
@@ -166,8 +163,8 @@
     for k in (4, 3, 5, 2, 6, 1, 7):
         z_copy(k).start()
 
-    for n in range(2, NC):
-        screen(n)
+    for n in range(4, NC):
+        screen(n, False)
 
     def spread_mask(c, _):
         for r in range(3):
@@ -250,42 +247,44 @@
             for d in range(2):
                 d_copy(g, d, s).wait_recv()
 
-    for n in range(4):
+    for n in range(3):
         spread(n)
     reduce_z()
+    for n in range(4, NC):
+        x_copy(n).start()
+    for n in range(1, NC):
+        b_copy(n).start()
+    spread(3)
+    reduce_x()
+    begin(0)
     spread(4)
+    onward(0, 1)
+    begin(1)
     spread(5)
     spread(6)
-    reduce_x()
-    begin(0)
-    begin(1)
-    for n in range(NC):
-        b_copy(n).start()
-    onward(0, 1)
+    onward(0, 2)
     onward(1, 1)
-    onward(0, 2)
     partner_on(0)
+    onward(0, 3)
     onward(1, 2)
     partner_on(1)
-    onward(0, 3)
     partner_on(2)
-    onward(1, 3)
     onward(0, 4)
     partner_on(3)
-    onward(1, 4)
+    onward(1, 3)
     partner_on(4)
-    partner_on(5)
-    partner_on(6)
     load_bare.wait()
     m_copy.wait_recv()
     gathered(0)
-    gathered(1)
+    onward(1, 4)
+    partner_on(5)
+    partner_on(6)
 
     energy = pair[0]
 
     def rows_done(start, width, which):
         side = (1 - xh) if which == 0 else xh
-        source, target = (barep, op) if which == 0 else (bareo, oo)
+        source = barep if which == 0 else bareo
         total = jnp.dot(wf[side].reshape(ROWS, NV), sfull[:, pl.ds(al(start), width)], preferred_element_type=F32)
         for c in range(width // TILE):
             at = pl.ds(al(start + c * TILE), TILE)
@@ -295,7 +294,11 @@
                 rows = slice(r * TILE, (r + 1) * TILE)
                 denom = (rowe[side, r] + line) - energy
                 value = source[rows, at].astype(F32) + total[rows, c * TILE:(c + 1) * TILE]
-                target[rows, at] = (value / denom * mv[which, r, pl.ds(column, 1), :]).astype(BF)
+                value = (value / denom * mv[which, r, pl.ds(column, 1), :]).astype(BF)
+                if which == 0:
+                    op[rows, at] = value
+                else:
+                    out[rows, pl.ds(al(mine + start + c * TILE), TILE)] = value
 
     def theirs_done(n, start, width):
         y_copy(0, 1, n).wait_recv()
@@ -308,9 +311,9 @@
 
     def mine_done(n):
         rows_done(n * WIDE, WIDE, 1)
-        own_out(n).start()
 
     theirs_done(0, 0, WIDE)
+    gathered(1)
 
     def work(n, _):
         theirs_done(n, n * WIDE, WIDE)
@@ -323,8 +326,6 @@
     theirs_done(6, STARTS[6], WIDTHS[6])
     mine_done(5)
 
-    for n in range(6):
-        own_out(n).wait()
     for j in range(3):
         t_copy(j).wait_send()
         i_copy(j).wait_send()
@@ -358,18 +359,18 @@
     smem = pl.BlockSpec(memory_space=pltpu.SMEM)
     inside = pl.BlockSpec(memory_space=pltpu.VMEM)
     sizes = [(NC,), (2, 2, NC), (2, NC), (NC,), (NC,)]
-    sems = [dma(size) for size in sizes for _ in range(2)] + [dma((6,)), dma, dma]
+    sems = [dma(size) for size in sizes for _ in range(2)] + [dma, dma]
     sems += [dma(size) for size in [(3,), (3,), (7,), (3,), (2, 2, 4), (2, 9)] for _ in range(2)]
     result = pl.pallas_call(
         kernel,
-        out_shape=jax.ShapeDtypeStruct((ROWS, NV), BF),
+        out_shape=vmem((ROWS, NV), BF),
         in_specs=[anywhere, smem, anywhere, inside, smem, inside, smem],
-        out_specs=anywhere,
+        out_specs=inside,
         scratch_shapes=[
             vmem((ROWS, NV), BF), vmem((NV, HALF), BF), vmem((ROWS, HALF), BF), vmem((ROWS, HALF), BF),
             vmem((ROWS, HALF), BF), pltpu.SMEM((4, TILE), jnp.int32), vmem((4, SLOTS + 1, QR, TILE), BF),
             vmem((3 * QR, NV), BF), vmem((7, 3 * QR, ZC), BF), vmem((3 * QR, ZC), BF), vmem((3, 3 * QR, ZC), BF),
-            vmem((2, 3, 4, QR, NV), BF), vmem((ROWS, HALF), BF), vmem((ROWS, HALF), BF),
+            vmem((2, 3, 4, QR, NV), BF), vmem((ROWS, HALF), BF),
             vmem((2, 3, TILE, TILE), F32), vmem((2, 3, NT, TILE), F32),
             dma((3,)), *sems,
         ],

time: 105 us -> 100 us (0.952)
  Pallas kernels: 99.6 us -> 97.3 us
  local copies, waits for them, and re-layouts: 3.22 us -> 1.41 us
    pallas_call x1, Pallas kernels: 99.6 us -> 97.3 us  [local(): pl.pallas_call(kernel, out_shape=vmem((ROWS, NV), BF), in_specs=[anywhere...]
    unnamed x1, local copies, waits for them, and re-layouts: 3.22 us -> 1.41 us
where the time goes in v3:
time: 100 us; the launch traced here: 99.3 us
  Pallas kernels  97.3 us (97%)
  local copies, waits for them, and re-layouts  1.41 us (1%)
    pallas_call x1, Pallas kernels, local(): pl.pallas_call(kernel, out_shape=vmem((ROWS, NV), BF), in_specs=[anywhere...  97.3 us

profile of v3, /device:TPU:2, one launch (start us, length us, event | category | flops | bytes accessed | tf_op | source)
XLA Modules:
  0.0 99.3 jit_solution(2157639826723170083)
XLA Ops:
  0.7 97.3 %cycle.1 = bf16[384,3072]{1,0:T(8,128)(2,1)S(1)} custom-call(bf16[384,3072]{1,0:T(8,128)(2,1)} %bitcast.8, s32[3,1,24]{2,1,0:T(1,128)} %bitcast.12, bf16[384,3072]{1,0:T(8,128)(2,1)} %bitcast.9, bf16[10,128,128]{2,1,0:T(8,128)(2,1)} %bitcast.10, s32[10]{0:T(128)} %bitcast.13, f32[24,128]{1,0:T(8,128)} %bitcast.11, f32[1]{0:T(128)S(6)} %copy.10.pair), custom_call_target="tpu_custom_call" | custom-call | tf_op jit(solution)/shard_map/cycle/pallas_call | solution.py:364
  97.9 1.4 %copy.9 = bf16[1,384,3072]{2,1,0:T(8,128)(2,1)} copy(bf16[1,384,3072]{2,1,0:T(8,128)(2,1)S(1)} %bitcast.7) | data formatting | bytes 4718592

commit v4 on v3

--- a/solution.py
+++ b/solution.py
@@ -26,8 +26,8 @@
     return pl.multiple_of(value, multiple)
 
 
-def kernel(amp, mask, bare, tiles, ids, eps, pair, out,
-           amps, sfull, ssend, barep, bareo, inv, tr, grid, zr, xsend, xr, wf, op, rowe, mv,
+def kernel(amp, mask_in, bare, tiles, ids_in, eps_in, pair_in, out,
+           amps, sfull, ssend, barep, bareo, inv, tr, grid, zr, xsend, xr, wf, op, rowe, mv, mask, ids, eps, pair,
            loc, sx, rx, sy, ry, sf, rf, sb, rb, so, ro, sm, rm, si, ri, st, rt, sz, rz, sw, rw, sa, ra, sd, rd):
     own, blk = lax.axis_index("own"), lax.axis_index("blk")
     core, z, xl = own % 2, (own // 2) % 8, own // 16
@@ -60,14 +60,20 @@
     load_theirs = pltpu.make_async_copy(amp.at[:, pl.ds(theirs, HALF)], amps.at[:, pl.ds(0, HALF)], loc.at[0])
     load_mine = pltpu.make_async_copy(amp.at[:, pl.ds(mine, HALF)], amps.at[:, pl.ds(HALF, HALF)], loc.at[1])
     load_bare = pltpu.make_async_copy(bare.at[:, pl.ds(mine, HALF)], bareo, loc.at[2])
-    load_theirs.start()
-    load_mine.start()
-    load_bare.start()
+    load_tiles = pltpu.make_async_copy(
+        tiles.at[:, pl.ds(al(quarter * QR, QR), QR), :], tr.at[0, pl.ds(0, SLOTS)], loc.at[3])
+    load_ids = pltpu.make_async_copy(ids_in, ids, loc.at[4])
+    load_mask = pltpu.make_async_copy(mask_in, mask, loc.at[5])
+    load_eps = pltpu.make_async_copy(eps_in, eps, loc.at[6])
+    load_pair = pltpu.make_async_copy(pair_in, pair, loc.at[7])
 
     barrier = pltpu.get_barrier_semaphore()
     peers = yn + zk + xs + [sibling, quad[2]]
     for peer in peers:
         pl.semaphore_signal(barrier, inc=1, device_id=peer, device_id_type=MESH)
+    for load in (load_ids, load_mask, load_theirs, load_mine, load_tiles, load_eps, load_pair, load_bare):
+        load.start()
+    load_ids.wait()
 
     def invert(q, _):
         slot = SLOTS
@@ -133,14 +139,14 @@
         y_copy(0, 0, n).start()
         y_copy(0, 1, n).start()
 
+    load_mask.wait()
     load_theirs.wait()
     load_mine.wait()
     for n in range(4):
         screen(n)
     b_copy(0).start()
 
-    for s in range(SLOTS):
-        tr[0, s] = tiles[s, pl.ds(al(quarter * QR, QR), QR), :]
+    load_tiles.wait()
     for j in range(4):
         tr[j, SLOTS] = jnp.zeros((QR, TILE), BF)
     for j in range(3):
@@ -175,21 +181,26 @@
     m_copy = remote(mv.at[1], mv.at[0], sm, rm, other)
     m_copy.start()
 
+    load_eps.wait()
+    load_pair.wait()
     for side in range(2):
         for r in range(3):
             line = eps[pl.ds((side * 4 + y) * 3 + r, 1), :]
             rowe[side, r] = jnp.transpose(jnp.broadcast_to(line, (TILE, TILE)))
 
-    def spread(n):
+    def spread(n, both=False):
         x_copy(n).wait_recv()
         y_copy(1, 0, n).start()
-        y_copy(1, 1, n).start()
+        if both:
+            y_copy(1, 1, n).start()
         y_copy(0, 0, n).wait_recv()
         f_copy(0, n).start()
 
     def partner_on(n):
         y_copy(1, 1, n).wait_recv()
         f_copy(1, n).start()
+        if n + 2 < NC:
+            y_copy(1, 1, n + 2).start()
 
     def w_copy(k):
         return remote(xsend, xr.at[k], sw.at[k], rw.at[k], xs[k])
@@ -247,38 +258,33 @@
             for d in range(2):
                 d_copy(g, d, s).wait_recv()
 
-    for n in range(3):
-        spread(n)
+    spread(0, True)
+    spread(1, True)
+    spread(2)
+    spread(3)
     reduce_z()
     for n in range(4, NC):
         x_copy(n).start()
     for n in range(1, NC):
         b_copy(n).start()
-    spread(3)
     reduce_x()
     begin(0)
+    partner_on(0)
     spread(4)
     onward(0, 1)
     begin(1)
     spread(5)
     spread(6)
+    partner_on(1)
     onward(0, 2)
     onward(1, 1)
-    partner_on(0)
+    partner_on(2)
     onward(0, 3)
     onward(1, 2)
-    partner_on(1)
-    partner_on(2)
     onward(0, 4)
-    partner_on(3)
-    onward(1, 3)
-    partner_on(4)
     load_bare.wait()
     m_copy.wait_recv()
     gathered(0)
-    onward(1, 4)
-    partner_on(5)
-    partner_on(6)
 
     energy = pair[0]
 
@@ -312,18 +318,21 @@
     def mine_done(n):
         rows_done(n * WIDE, WIDE, 1)
 
-    theirs_done(0, 0, WIDE)
-    gathered(1)
-
-    def work(n, _):
-        theirs_done(n, n * WIDE, WIDE)
-        mine_done(n - 1)
-        return 0
-
-    lax.fori_loop(1, 5, work, 0)
-    theirs_done(5, STARTS[5], WIDTHS[5])
-    mine_done(4)
-    theirs_done(6, STARTS[6], WIDTHS[6])
+    for n in range(NC):
+        theirs_done(n, STARTS[n], WIDTHS[n])
+        if n == 0:
+            partner_on(3)
+            onward(1, 3)
+        elif n == 1:
+            onward(1, 4)
+            gathered(1)
+        elif n < 5:
+            mine_done(n - 2)
+            partner_on(n + 2)
+            if n == 4:
+                mine_done(3)
+        elif n == 5:
+            mine_done(4)
     mine_done(5)
 
     for j in range(3):
@@ -356,7 +365,6 @@
     dma = pltpu.SemaphoreType.DMA
     vmem = pltpu.VMEM
     anywhere = pl.BlockSpec(memory_space=pl.ANY)
-    smem = pl.BlockSpec(memory_space=pltpu.SMEM)
     inside = pl.BlockSpec(memory_space=pltpu.VMEM)
     sizes = [(NC,), (2, 2, NC), (2, NC), (NC,), (NC,)]
     sems = [dma(size) for size in sizes for _ in range(2)] + [dma, dma]
@@ -364,7 +372,7 @@
     result = pl.pallas_call(
         kernel,
         out_shape=vmem((ROWS, NV), BF),
-        in_specs=[anywhere, smem, anywhere, inside, smem, inside, smem],
+        in_specs=[anywhere] * 7,
         out_specs=inside,
         scratch_shapes=[
             vmem((ROWS, NV), BF), vmem((NV, HALF), BF), vmem((ROWS, HALF), BF), vmem((ROWS, HALF), BF),
@@ -372,7 +380,8 @@
             vmem((3 * QR, NV), BF), vmem((7, 3 * QR, ZC), BF), vmem((3 * QR, ZC), BF), vmem((3, 3 * QR, ZC), BF),
             vmem((2, 3, 4, QR, NV), BF), vmem((ROWS, HALF), BF),
             vmem((2, 3, TILE, TILE), F32), vmem((2, 3, NT, TILE), F32),
-            dma((3,)), *sems,
+            pltpu.SMEM((3, 1, NT), jnp.int32), pltpu.SMEM((SLOTS,), jnp.int32), vmem((NT, TILE), F32), pltpu.SMEM((1,), F32),
+            dma((8,)), *sems,
         ],
         compiler_params=pltpu.CompilerParams(
             collective_id=0, has_side_effects=True, vmem_limit_bytes=56 * 1024 * 1024),

time: 100 us -> 98.7 us (0.987)
  Pallas kernels: 97.3 us -> 95.7 us
    pallas_call x1, Pallas kernels: 97.3 us -> 95.7 us  [local(): pl.pallas_call(kernel, out_shape=vmem((ROWS, NV), BF), in_specs=[anywhere...]
where the time goes in v4:
time: 98.7 us; the launch traced here: 97.7 us
  Pallas kernels  95.7 us (97%)
  local copies, waits for them, and re-layouts  1.41 us (1%)
    pallas_call x1, Pallas kernels, local(): pl.pallas_call(kernel, out_shape=vmem((ROWS, NV), BF), in_specs=[anywhere...  95.7 us

profile of v4, /device:TPU:2, one launch (start us, length us, event | category | flops | bytes accessed | tf_op | source)
XLA Modules:
  0.0 97.7 jit_solution(8402374540268086018)
XLA Ops:
  0.7 95.7 %cycle.1 = bf16[384,3072]{1,0:T(8,128)(2,1)S(1)} custom-call(bf16[384,3072]{1,0:T(8,128)(2,1)} %bitcast.8, s32[3,1,24]{2,1,0:T(1,128)} %bitcast.12, bf16[384,3072]{1,0:T(8,128)(2,1)} %bitcast.9, bf16[10,128,128]{2,1,0:T(8,128)(2,1)} %bitcast.10, s32[10]{0:T(128)} %bitcast.13, f32[24,128]{1,0:T(8,128)} %bitcast.11, f32[1]{0:T(128)S(6)} %copy.10.pair_in), custom_call_target="tpu_custom_call" | custom-call | tf_op jit(solution)/shard_map/cycle/pallas_call | solution.py:372
  96.3 1.4 %copy.9 = bf16[1,384,3072]{2,1,0:T(8,128)(2,1)} copy(bf16[1,384,3072]{2,1,0:T(8,128)(2,1)S(1)} %bitcast.7) | data formatting | bytes 4718592

commit v5 on v4

--- a/solution.py
+++ b/solution.py
@@ -13,8 +13,8 @@
 HALF = 1536
 QR = 32
 ZC = 384
-STARTS = (0, 256, 512, 768, 1024, 1280, 1408)
-WIDTHS = (256, 256, 256, 256, 256, 128, 128)
+STARTS = (0, 256, 512, 768, 1024, 1152, 1280, 1408)
+WIDTHS = (256, 256, 256, 256, 128, 128, 128, 128)
 NC = len(STARTS)
 WIDE = 256
 MESH = pl.DeviceIdType.MESH
@@ -28,7 +28,7 @@
 
 def kernel(amp, mask_in, bare, tiles, ids_in, eps_in, pair_in, out,
            amps, sfull, ssend, barep, bareo, inv, tr, grid, zr, xsend, xr, wf, op, rowe, mv, mask, ids, eps, pair,
-           loc, sx, rx, sy, ry, sf, rf, sb, rb, so, ro, sm, rm, si, ri, st, rt, sz, rz, sw, rw, sa, ra, sd, rd):
+           loc, lx, sx, rx, sy, ry, sf, rf, sb, rb, so, ro, sm, rm, si, ri, st, rt, sz, rz, sw, rw, sa, ra, sd, rd):
     own, blk = lax.axis_index("own"), lax.axis_index("blk")
     core, z, xl = own % 2, (own // 2) % 8, own // 16
     xh, y = blk // 4, blk % 4
@@ -57,8 +57,13 @@
     quarters = [(1 - core) * 2 + xl, core * 2 + 1 - xl, (1 - core) * 2 + 1 - xl]
 
     mine, theirs = al(xh * HALF), al((1 - xh) * HALF)
-    load_theirs = pltpu.make_async_copy(amp.at[:, pl.ds(theirs, HALF)], amps.at[:, pl.ds(0, HALF)], loc.at[0])
-    load_mine = pltpu.make_async_copy(amp.at[:, pl.ds(mine, HALF)], amps.at[:, pl.ds(HALF, HALF)], loc.at[1])
+
+    def load_amps(side, n):
+        first = theirs if side == 0 else mine
+        return pltpu.make_async_copy(
+            amp.at[:, pl.ds(al(first + STARTS[n]), WIDTHS[n])],
+            amps.at[:, pl.ds(side * HALF + STARTS[n], WIDTHS[n])], lx.at[side, n])
+
     load_bare = pltpu.make_async_copy(bare.at[:, pl.ds(mine, HALF)], bareo, loc.at[2])
     load_tiles = pltpu.make_async_copy(
         tiles.at[:, pl.ds(al(quarter * QR, QR), QR), :], tr.at[0, pl.ds(0, SLOTS)], loc.at[3])
@@ -71,7 +76,14 @@
     peers = yn + zk + xs + [sibling, quad[2]]
     for peer in peers:
         pl.semaphore_signal(barrier, inc=1, device_id=peer, device_id_type=MESH)
-    for load in (load_ids, load_mask, load_theirs, load_mine, load_tiles, load_eps, load_pair, load_bare):
+    load_mask.start()
+    load_ids.start()
+    for n in range(NC):
+        for side in range(2):
+            load_amps(side, n).start()
+        if n == 1:
+            load_tiles.start()
+    for load in (load_eps, load_pair, load_bare):
         load.start()
     load_ids.wait()
 
@@ -83,48 +95,13 @@
         return 0
 
     lax.fori_loop(0, 3 * NT, invert, 0)
-    pl.semaphore_wait(barrier, len(peers))
-
-    def rows_of(xh_, y_):
-        return pl.ds(al((xh_ * 4 + y_) * ROWS), ROWS)
-
-    def part(n, base=0):
-        if isinstance(n, int):
-            return pl.ds(al(base + STARTS[n]), WIDTHS[n])
-        return pl.ds(al(base + n * WIDE), WIDE)
-
-    def x_copy(n):
-        return remote(ssend.at[:, part(n)], sfull.at[rows_of(xh, y), part(n)], sx.at[n], rx.at[n], other)
-
-    def y_copy(b, d, n):
-        where = sfull.at[rows_of(xh if b == 0 else 1 - xh, y), part(n)]
-        return remote(where, where, sy.at[b, d, n], ry.at[b, d, n], yn[d])
-
-    def f_copy(d, n):
-        where = sfull.at[rows_of(xh if d == 0 else 1 - xh, (y + 3) % 4 if d == 0 else (y + 1) % 4), part(n)]
-        return remote(where, where, sf.at[d, n], rf.at[d, n], yn[d])
-
-    def b_copy(n):
-        return remote(bare.at[:, part(n, theirs)], barep.at[:, part(n)], sb.at[n], rb.at[n], other)
-
-    def o_copy(n):
-        return remote(op.at[:, part(n)], out.at[:, part(n, mine)], so.at[n], ro.at[n], other)
-
-    def t_copy(j):
-        return remote(tiles.at[:, pl.ds(al(quarters[j] * QR, QR), QR), :], tr.at[j + 1, pl.ds(0, SLOTS)], st.at[j], rt.at[j], quad[j])
-
-    def i_copy(j):
-        return remote(inv.at[0], inv.at[j + 1], si.at[j], ri.at[j], quad[j])
-
-    for j in range(3):
-        t_copy(j).start()
-        i_copy(j).start()
-
-    def screen(n, send=True):
-        count = WIDTHS[n] // TILE
+
+    def screen(n):
+        load_amps(0, n).wait()
+        load_amps(1, n).wait()
         for side in range(2):
             first = (1 - xh) if side == 0 else xh
-            for c in range(count):
+            for c in range(WIDTHS[n] // TILE):
                 here = STARTS[n] + c * TILE
                 for r in range(3):
                     keep = mask[r, 0, first * (NT // 2) + here // TILE]
@@ -134,16 +111,56 @@
                         ssend[r * TILE:(r + 1) * TILE, here:here + TILE] = tile
                     else:
                         sfull[pl.ds(al(blk * ROWS + r * TILE), TILE), here:here + TILE] = tile
-            if side == 0 and send:
-                x_copy(n).start()
+
+    load_mask.wait()
+    screen(0)
+    pl.semaphore_wait(barrier, len(peers))
+
+    def rows_of(xh_, y_):
+        return pl.ds(al((xh_ * 4 + y_) * ROWS), ROWS)
+
+    def part(n, base=0):
+        if isinstance(n, int):
+            return pl.ds(al(base + STARTS[n]), WIDTHS[n])
+        return pl.ds(al(base + n * WIDE), WIDE)
+
+    def x_copy(n):
+        return remote(ssend.at[:, part(n)], sfull.at[rows_of(xh, y), part(n)], sx.at[n], rx.at[n], other)
+
+    def y_copy(b, d, n):
+        where = sfull.at[rows_of(xh if b == 0 else 1 - xh, y), part(n)]
+        return remote(where, where, sy.at[b, d, n], ry.at[b, d, n], yn[d])
+
+    def f_copy(d, n):
+        where = sfull.at[rows_of(xh if d == 0 else 1 - xh, (y + 3) % 4 if d == 0 else (y + 1) % 4), part(n)]
+        return remote(where, where, sf.at[d, n], rf.at[d, n], yn[d])
+
+    def b_copy(n):
+        return remote(bare.at[:, part(n, theirs)], barep.at[:, part(n)], sb.at[n], rb.at[n], other)
+
+    def o_copy(n):
+        return remote(op.at[:, part(n)], out.at[:, part(n, mine)], so.at[n], ro.at[n], other)
+
+    def t_copy(j):
+        return remote(tiles.at[:, pl.ds(al(quarters[j] * QR, QR), QR), :], tr.at[j + 1, pl.ds(0, SLOTS)], st.at[j], rt.at[j], quad[j])
+
+    def i_copy(j):
+        return remote(inv.at[0], inv.at[j + 1], si.at[j], ri.at[j], quad[j])
+
+    for j in range(3):
+        t_copy(j).start()
+        i_copy(j).start()
+
+    def send(n, across=True):
+        if across:
+            x_copy(n).start()
         y_copy(0, 0, n).start()
         y_copy(0, 1, n).start()
 
-    load_mask.wait()
-    load_theirs.wait()
-    load_mine.wait()
-    for n in range(4):
+    send(0)
+    for n in range(1, 4):
         screen(n)
+        send(n)
     b_copy(0).start()
 
     load_tiles.wait()
@@ -170,7 +187,8 @@
         z_copy(k).start()
 
     for n in range(4, NC):
-        screen(n, False)
+        screen(n)
+        send(n, False)
 
     def spread_mask(c, _):
         for r in range(3):
@@ -275,6 +293,7 @@
     begin(1)
     spread(5)
     spread(6)
+    spread(7)
     partner_on(1)
     onward(0, 2)
     onward(1, 1)
@@ -286,12 +305,13 @@
     m_copy.wait_recv()
     gathered(0)
 
-    energy = pair[0]
-
-    def rows_done(start, width, which):
+    energy = pair[0, 0]
+
+    def rows_done(start, width, which, total=None):
         side = (1 - xh) if which == 0 else xh
         source = barep if which == 0 else bareo
-        total = jnp.dot(wf[side].reshape(ROWS, NV), sfull[:, pl.ds(al(start), width)], preferred_element_type=F32)
+        if total is None:
+            total = jnp.dot(wf[side].reshape(ROWS, NV), sfull[:, pl.ds(al(start), width)], preferred_element_type=F32)
         for c in range(width // TILE):
             at = pl.ds(al(start + c * TILE), TILE)
             column = xh * (NT // 2) + start // TILE + c
@@ -318,7 +338,7 @@
     def mine_done(n):
         rows_done(n * WIDE, WIDE, 1)
 
-    for n in range(NC):
+    for n in range(NC - 1):
         theirs_done(n, STARTS[n], WIDTHS[n])
         if n == 0:
             partner_on(3)
@@ -326,26 +346,24 @@
         elif n == 1:
             onward(1, 4)
             gathered(1)
-        elif n < 5:
+        elif n < 6:
             mine_done(n - 2)
             partner_on(n + 2)
-            if n == 4:
-                mine_done(3)
-        elif n == 5:
-            mine_done(4)
-    mine_done(5)
-
-    for j in range(3):
-        t_copy(j).wait_send()
-        i_copy(j).wait_send()
-    m_copy.wait_send()
-    for n in range(NC):
+
+    def sent(n):
         x_copy(n).wait_send()
         b_copy(n).wait_send()
         for d in range(2):
             y_copy(0, d, n).wait_send()
             y_copy(1, d, n).wait_send()
             f_copy(d, n).wait_send()
+
+    for j in range(3):
+        t_copy(j).wait_send()
+        i_copy(j).wait_send()
+    m_copy.wait_send()
+    for n in range(NC - 2):
+        sent(n)
     for k in range(1, 8):
         z_copy(k).wait_send()
     for k in range(3):
@@ -356,6 +374,30 @@
             for t in range(4):
                 a_copy(g, d, t).wait_send()
                 d_copy(g, d, t + 1).wait_send()
+
+    last = NC - 1
+    y_copy(0, 1, last).wait_recv()
+    y_copy(1, 0, last).wait_recv()
+    b_copy(last).wait_recv()
+
+    def block_dot(xh_, y_):
+        rows = rows_of(xh_, y_)
+        return jnp.dot(wf[1 - xh, :, :, :, rows].reshape(ROWS, ROWS), sfull[rows, part(last)], preferred_element_type=F32)
+
+    total = block_dot(0, y) + block_dot(1, y)
+    for step in (1, 3):
+        total = total + block_dot(0, (y + step) % 4) + block_dot(1, (y + step) % 4)
+    for d in range(2):
+        f_copy(d, last).wait_recv()
+    for d in range(2):
+        total = total + block_dot(d, (y + 2) % 4)
+    rows_done(STARTS[last], WIDTHS[last], 0, total)
+    o_copy(last).start()
+    mine_done(4)
+    mine_done(5)
+
+    sent(NC - 2)
+    sent(NC - 1)
     for n in range(NC):
         o_copy(n).wait_send()
         o_copy(n).wait_recv()
@@ -380,14 +422,14 @@
             vmem((3 * QR, NV), BF), vmem((7, 3 * QR, ZC), BF), vmem((3 * QR, ZC), BF), vmem((3, 3 * QR, ZC), BF),
             vmem((2, 3, 4, QR, NV), BF), vmem((ROWS, HALF), BF),
             vmem((2, 3, TILE, TILE), F32), vmem((2, 3, NT, TILE), F32),
-            pltpu.SMEM((3, 1, NT), jnp.int32), pltpu.SMEM((SLOTS,), jnp.int32), vmem((NT, TILE), F32), pltpu.SMEM((1,), F32),
-            dma((8,)), *sems,
+            pltpu.SMEM((3, 1, NT), jnp.int32), pltpu.SMEM((SLOTS,), jnp.int32), vmem((NT, TILE), F32), pltpu.SMEM((1, 1), F32),
+            dma((8,)), dma((2, NC)), *sems,
         ],
         compiler_params=pltpu.CompilerParams(
             collective_id=0, has_side_effects=True, vmem_limit_bytes=56 * 1024 * 1024),
         name="cycle",
     )(amplitudes.reshape(ROWS, NV), amp_mask.reshape(3, 1, NT), bare_ints.reshape(ROWS, NV),
-      int_tiles.reshape(SLOTS, TILE, TILE), tile_ids.reshape(SLOTS), eps_virt.reshape(NT, TILE), eps_pair)
+      int_tiles.reshape(SLOTS, TILE, TILE), tile_ids.reshape(SLOTS), eps_virt.reshape(NT, TILE), eps_pair.reshape(1, 1))
     return result.reshape(1, ROWS, NV)
 
 

time: 98.7 us -> 99 us (level)
  no operation moved by 1% of the time
where the time goes in v5:
time: 99 us; the launch traced here: 98 us
  Pallas kernels  96 us (97%)
  local copies, waits for them, and re-layouts  1.41 us (1%)
    pallas_call x1, Pallas kernels, local(): pl.pallas_call(kernel, out_shape=vmem((ROWS, NV), BF), in_specs=[anywhere...  96 us

profile of v5, /device:TPU:2, one launch (start us, length us, event | category | flops | bytes accessed | tf_op | source)
XLA Modules:
  0.0 98.0 jit_solution(10575749120658921932)
XLA Ops:
  0.7 96.0 %cycle.1 = bf16[384,3072]{1,0:T(8,128)(2,1)S(1)} custom-call(bf16[384,3072]{1,0:T(8,128)(2,1)} %bitcast.10, s32[3,1,24]{2,1,0:T(1,128)} %bitcast.14, bf16[384,3072]{1,0:T(8,128)(2,1)} %bitcast.11, bf16[10,128,128]{2,1,0:T(8,128)(2,1)} %bitcast.12, s32[10]{0:T(128)} %bitcast.15, f32[24,128]{1,0:T(8,128)} %bitcast.13, f32[1,1]{1,0:T(1,128)} %bitcast.8.pair_in), custom_call_target="tpu_custom_call" | custom-call | tf_op jit(solution)/shard_map/cycle/pallas_call | solution.py:414
  96.6 1.4 %copy.9 = bf16[1,384,3072]{2,1,0:T(8,128)(2,1)} copy(bf16[1,384,3072]{2,1,0:T(8,128)(2,1)S(1)} %bitcast.9) | data formatting | bytes 4718592
